TPU v7x, 256 devices: a whole 4x4x8 slice. The times are simulated.
256 devices in a mesh: node: 16 (over z, core), head: 16 (over x, y).
Axes of the slice: x: 4, y: 4, z: 8, core: 2. Of those that a mesh axis runs over, the one named last changes fastest.
Arguments:
- features: bfloat16 [65536, 1024], P(('node', 'head')), may hold values from -6 to 6
- attn_gain: float32 [1024], replicated, may hold values from 0.25 to 1.75
- qkv_weight: bfloat16 [1024, 16, 192], P(None, 'head')
- out_weight: bfloat16 [1024, 1024], replicated, may hold values from -0.1875 to 0.1875
- feedforward_norm_gain: float32 [1024], replicated, may hold values from 0.25 to 1.75
- up_weight: bfloat16 [1024, 2048], replicated, may hold values from -0.1875 to 0.1875
- down_weight: bfloat16 [2048, 1024], replicated, may hold values from -0.125 to 0.125
- tile_pattern: int32 [512, 8], P('node'), may hold values from 0 to 511, as said below
- node_order: int32 [16, 4096], P('node'), may hold values from 0 to 4095, each once within a row
Outputs:
- updated: bfloat16 [65536, 1024], P(('node', 'head'))
Inputs may be any that keep to these rules, and one draw needn't show every extreme that they name: `tile_pattern`: row t names 8 different tiles; the first is t itself; all lie in partitions (tiles p * 32 to (p + 1) * 32 - 1) at cyclic distance at most 2 from t's partition; the second lies 2 partitions below t's and the third 2 above. `node_order`: each row lists every local row of its partition once.
All inputs are finite; a program needn't handle non-finite values.
Results may differ from a plain program's by a relative error of at most 0.0045.
Values may be sent and summed in bfloat16 or wider, within the bound.
A program may use at most 64 MiB of HBM per device.

v0:
```python
import math

import jax
import jax.numpy as jnp
from jax import lax
from jax.sharding import PartitionSpec as P

D = 1024
HD = 64
TILE = 128
NNZ = 8
REACH = 2


def passed_along(x, axis, by):
    size = lax.axis_size(axis)
    return lax.ppermute(x, axis, [(i, (i + by) % size) for i in range(size)])


def layer_norm(values, gain):
    row_mean = jnp.mean(values, -1, keepdims=True)
    centred = values - row_mean
    variance = jnp.mean(centred * centred, -1, keepdims=True)
    return centred * lax.rsqrt(variance + 1e-05) * gain


def shards(
    features,
    attn_gain,
    qkv_weight,
    out_weight,
    feedforward_norm_gain,
    up_weight,
    down_weight,
    tile_pattern,
    node_order,
):
    own_rows = features.shape[0]
    local_heads = qkv_weight.shape[1]
    head_placements = lax.axis_size("head")
    partitions = lax.axis_size("node")
    rows_part = own_rows * head_placements
    query_tiles = rows_part // TILE
    normed = layer_norm(features.astype(jnp.float32), attn_gain).astype(jnp.bfloat16)
    reordered_weight = jnp.concatenate([qkv_weight[:, :, HD:], qkv_weight[:, :, :HD]], -1)
    local_weight = reordered_weight.reshape(D, local_heads * 3 * HD)
    projected = jnp.dot(
        lax.all_gather(normed, "head", axis=0, tiled=True),
        local_weight,
        preferred_element_type=jnp.float32,
    ).astype(jnp.bfloat16)
    projected = projected.reshape(rows_part, local_heads, 3 * HD)
    partition_permutation = node_order[0]
    keyval_rows = projected[:, :, : 2 * HD].reshape(rows_part, local_heads * 2 * HD)
    query_rows = projected[:, :, 2 * HD :].reshape(rows_part, local_heads * HD)
    keyval = jnp.take(keyval_rows, partition_permutation, axis=0)
    queries = jnp.take(query_rows, partition_permutation, axis=0)
    current = passed_along(keyval, "node", -REACH)
    blocks = [current]
    for cycle_step in range(2 * REACH):
        current = passed_along(current, "node", 1)
        blocks.append(current)
    window = jnp.stack(blocks[::-1])
    window_tiles = window.reshape((2 * REACH + 1) * query_tiles, TILE, local_heads * 2 * HD)
    partition = lax.axis_index("node")
    window_position = (
        tile_pattern // query_tiles - partition + REACH + partitions
    ) % partitions * query_tiles + tile_pattern % query_tiles
    tile_group = math.gcd(query_tiles, max(1, 512 // TILE))
    score_scale = 1.0 / math.sqrt(HD)

    def attend(item_pair):
        group_queries, columns = item_pair
        picked = jnp.take(window_tiles, columns.reshape(tile_group * NNZ), axis=0)
        picked = picked.reshape(tile_group, NNZ * TILE, local_heads, 2 * HD)
        key_rows = picked[..., :HD]
        value_rows = picked[..., HD:]
        query_block = group_queries.reshape(tile_group, TILE, local_heads, HD)
        scores = (
            jnp.einsum("gqhd,gmhd->ghqm", query_block, key_rows, preferred_element_type=jnp.float32)
            * score_scale
        )
        row_max = jnp.max(scores, -1, keepdims=True)
        expd = jnp.exp(scores - row_max)
        weight_arrays = (expd / jnp.sum(expd, -1, keepdims=True)).astype(jnp.bfloat16)
        result = jnp.einsum(
            "ghqm,gmhd->gqhd", weight_arrays, value_rows, preferred_element_type=jnp.float32
        ).astype(jnp.bfloat16)
        return result.reshape(tile_group * TILE, local_heads * HD)

    grouped_queries = queries.reshape(
        query_tiles // tile_group, tile_group * TILE, local_heads * HD
    )
    grouped_slots = window_position.reshape(query_tiles // tile_group, tile_group, NNZ)
    attended = lax.map(attend, (grouped_queries, grouped_slots)).reshape(
        rows_part, local_heads * HD
    )
    inverse_order = (
        jnp.zeros((rows_part,), jnp.int32)
        .at[partition_permutation]
        .set(jnp.arange(rows_part, dtype=jnp.int32))
    )
    restored = jnp.take(attended, inverse_order, axis=0)
    gathered_heads = lax.all_to_all(restored, "head", split_axis=0, concat_axis=1, tiled=True)
    residual = features.astype(jnp.float32) + jnp.dot(
        gathered_heads, out_weight, preferred_element_type=jnp.float32
    )
    mlp_input = layer_norm(residual, feedforward_norm_gain).astype(jnp.bfloat16)
    hidden = jax.nn.gelu(jnp.dot(mlp_input, up_weight, preferred_element_type=jnp.float32)).astype(
        jnp.bfloat16
    )
    return (residual + jnp.dot(hidden, down_weight, preferred_element_type=jnp.float32)).astype(
        jnp.bfloat16
    )


def solution(mesh):
    return jax.shard_map(
        shards,
        mesh=mesh,
        in_specs=(
            P(("node", "head"), None),
            P(),
            P(None, "head", None),
            P(),
            P(),
            P(),
            P(),
            P("node", None),
            P("node", None),
        ),
        out_specs=P(("node", "head"), None),
        check_vma=False,
    )
```

profile of v0, /device:TPU:96, one launch (start us, length us, event | category | flops | bytes accessed | tf_op | source)
XLA Modules:
  0.0 371.6 jit_solution(18285803736506806688)
XLA Ops:
  9.3 2.1 fusion.37
  11.5 77.8 %all-gather.2.cloned.1.call-done = bf16[4096,1024]{1,0:T(8,128)(2,1)} async-done(((bf16[256,1024]{1,0:T(8,128)(2,1)}), bf16[4096,1024]{1,0:T(8,128)(2,1)}) %all-gather.2.cloned.1.call-update) | async-done | bytes 8388624 | tf_op jit(solution)/shard_map/all_gather | solution.py:48
  89.3 6.3 %fusion.23 = bf16[4096,1,192]{0,2,1:T(8,128)(2,1)S(1)} fusion(bf16[4096,1024]{1,0:T(8,128)(2,1)} %all-gather.2.cloned.1.call-done, bf16[1024,1,64]{0,2,1:T(8,128)(2,1)S(1)} %slice-done, bf16[1024,1,128]{0,2,1:T(8,128)(2,1)S(1)} %slice-done.1), kind=kOutput, calls=%fused_computation.33 | convolution fusion | flops 1612185600 | bytes 10354688 | tf_op jit(solution)/shard_map/dot_general | solution.py:47
  99.4 15.0 %gather_fusion.1 = bf16[4096,128]{1,0:T(8,128)(2,1)} fusion(bf16[4096,128]{1,0:T(8,128)(2,1)S(1)} %copy.17, s32[4096]{0:T(1024)S(1)} %broadcast_clamp_fusion), kind=kCustom, calls=%fused_computation.3 | custom fusion | bytes 2113536 | tf_op jit(solution)/shard_map/jit(_take)/gather | solution.py:56
  114.4 3.4 broadcast_select_fusion.3
  118.3 25.5 %collective-permute-done = bf16[4096,128]{1,0:T(8,128)(2,1)S(1)} collective-permute-done((bf16[4096,128]{1,0:T(8,128)(2,1)S(1)}, bf16[4096,128]{1,0:T(8,128)(2,1)S(1)}, u32[]{:S(2)}, u32[]{:S(2)}) %collective-permute-start) | collective-permute-done | bytes 1048608 | tf_op jit(solution)/shard_map/ppermute | solution.py:17
  144.8 14.2 %collective-permute-done.1 = bf16[4096,128]{1,0:T(8,128)(2,1)S(1)} collective-permute-done((bf16[4096,128]{1,0:T(8,128)(2,1)S(1)}, bf16[4096,128]{1,0:T(8,128)(2,1)S(1)}, u32[]{:S(2)}, u32[]{:S(2)}) %collective-permute-start.1) | collective-permute-done | bytes 1048608 | tf_op jit(solution)/shard_map/ppermute | solution.py:17
  160.0 14.2 %collective-permute-done.2 = bf16[4096,128]{1,0:T(8,128)(2,1)S(1)} collective-permute-done((bf16[4096,128]{1,0:T(8,128)(2,1)S(1)}, bf16[4096,128]{1,0:T(8,128)(2,1)S(1)}, u32[]{:S(2)}, u32[]{:S(2)}) %collective-permute-start.2) | collective-permute-done | bytes 1048608 | tf_op jit(solution)/shard_map/ppermute | solution.py:17
  174.7 15.7 %scatter_custom_fusion = s32[4096]{0:T(1024)S(1)} fusion(s32[4096]{0:T(1024)S(1)} %bitcast.103, s32[4096]{0:T(1024)S(1)} %iota.3, s32[]{:T(128)} %copy.60), kind=kCustom, calls=%fused_computation.84 | custom fusion | bytes 16388 | tf_op jit(solution)/shard_map/scatter | solution.py:101
  190.5 3.7 collective-permute-start.4
  197.6 15.0 %gather_fusion.2 = bf16[4096,64]{1,0:T(8,128)(2,1)} fusion(bf16[4096,64]{1,0:T(8,128)(2,1)S(1)} %copy.18, s32[4096]{0:T(1024)S(1)} %get-tuple-element.53), kind=kCustom, calls=%fused_computation.clone | custom fusion | bytes 1064960 | tf_op jit(solution)/shard_map/jit(_take)/gather | solution.py:57
  212.6 3.4 broadcast_select_fusion.2
  221.4 2.3 copy-done.3
  223.7 92.5 %while.10 = (s32[]{:T(128)}, bf16[8,512,64]{1,2,0:T(8,128)(2,1)}, s32[8,4,8]{2,1,0:T(4,128)S(1)}, bf16[160,128,128]{2,1,0:T(8,128)(2,1)}, bf16[8,512,64]{1,2,0:T(8,128)(2,1)}, /*index=5*/s32[]{:T(128)}) while((s32[]{:T(128)}, bf16[8,512,64]{1,2,0:T(8,128)(2,1)}, s32[8,4,8]{2,1,0:T(4,128)S(1)}, bf16[160,128,128]{2,1,0:T(8,128)(2,1)}, ...), condition=%wide.region_5.7_spmd, body=%wide.region_2.6_spmd.sunk | while | flops 205557536 | bytes 12936373 | solution.py:95
  224.7 4.2 %gather_fusion = bf16[32,128,128]{2,1,0:T(8,128)(2,1)} fusion(bf16[160,128,128]{2,1,0:T(8,128)(2,1)} %get-tuple-element.105, s32[1024]{0:T(1024)S(1)} %pad_clamp_fusion.2), kind=kCustom, calls=%fused_computation.1.clone.1 | custom fusion | bytes 2097280 | tf_op jit(solution)/shard_map/while/body/eval_jaxpr/jit(_take)/gather | solution.py:74
  231.5 2.0 fusion.86
  236.3 4.2 %gather_fusion = bf16[32,128,128]{2,1,0:T(8,128)(2,1)} fusion(bf16[160,128,128]{2,1,0:T(8,128)(2,1)} %get-tuple-element.105, s32[1024]{0:T(1024)S(1)} %pad_clamp_fusion.2), kind=kCustom, calls=%fused_computation.1.clone.1 | custom fusion | bytes 2097280 | tf_op jit(solution)/shard_map/while/body/eval_jaxpr/jit(_take)/gather | solution.py:74
  243.1 2.0 fusion.86
  247.9 4.2 %gather_fusion = bf16[32,128,128]{2,1,0:T(8,128)(2,1)} fusion(bf16[160,128,128]{2,1,0:T(8,128)(2,1)} %get-tuple-element.105, s32[1024]{0:T(1024)S(1)} %pad_clamp_fusion.2), kind=kCustom, calls=%fused_computation.1.clone.1 | custom fusion | bytes 2097280 | tf_op jit(solution)/shard_map/while/body/eval_jaxpr/jit(_take)/gather | solution.py:74
  259.4 4.2 %gather_fusion = bf16[32,128,128]{2,1,0:T(8,128)(2,1)} fusion(bf16[160,128,128]{2,1,0:T(8,128)(2,1)} %get-tuple-element.105, s32[1024]{0:T(1024)S(1)} %pad_clamp_fusion.2), kind=kCustom, calls=%fused_computation.1.clone.1 | custom fusion | bytes 2097280 | tf_op jit(solution)/shard_map/while/body/eval_jaxpr/jit(_take)/gather | solution.py:74
  266.2 2.0 fusion.86
  271.0 4.2 %gather_fusion = bf16[32,128,128]{2,1,0:T(8,128)(2,1)} fusion(bf16[160,128,128]{2,1,0:T(8,128)(2,1)} %get-tuple-element.105, s32[1024]{0:T(1024)S(1)} %pad_clamp_fusion.2), kind=kCustom, calls=%fused_computation.1.clone.1 | custom fusion | bytes 2097280 | tf_op jit(solution)/shard_map/while/body/eval_jaxpr/jit(_take)/gather | solution.py:74
  277.8 2.0 fusion.86
  282.5 4.2 %gather_fusion = bf16[32,128,128]{2,1,0:T(8,128)(2,1)} fusion(bf16[160,128,128]{2,1,0:T(8,128)(2,1)} %get-tuple-element.105, s32[1024]{0:T(1024)S(1)} %pad_clamp_fusion.2), kind=kCustom, calls=%fused_computation.1.clone.1 | custom fusion | bytes 2097280 | tf_op jit(solution)/shard_map/while/body/eval_jaxpr/jit(_take)/gather | solution.py:74
  289.3 2.0 fusion.86
  294.1 4.2 %gather_fusion = bf16[32,128,128]{2,1,0:T(8,128)(2,1)} fusion(bf16[160,128,128]{2,1,0:T(8,128)(2,1)} %get-tuple-element.105, s32[1024]{0:T(1024)S(1)} %pad_clamp_fusion.2), kind=kCustom, calls=%fused_computation.1.clone.1 | custom fusion | bytes 2097280 | tf_op jit(solution)/shard_map/while/body/eval_jaxpr/jit(_take)/gather | solution.py:74
  305.7 4.2 %gather_fusion = bf16[32,128,128]{2,1,0:T(8,128)(2,1)} fusion(bf16[160,128,128]{2,1,0:T(8,128)(2,1)} %get-tuple-element.105, s32[1024]{0:T(1024)S(1)} %pad_clamp_fusion.2), kind=kCustom, calls=%fused_computation.1.clone.1 | custom fusion | bytes 2097280 | tf_op jit(solution)/shard_map/while/body/eval_jaxpr/jit(_take)/gather | solution.py:74
  312.5 2.0 fusion.86
  317.7 15.0 %gather_fusion.3 = bf16[4096,64]{1,0:T(8,128)(2,1)} fusion(bf16[4096,64]{1,0:T(8,128)(2,1)S(1)} %bitcast.94, s32[4096]{0:T(1024)S(1)} %get-tuple-element.54), kind=kCustom, calls=%fused_computation.2.clone | custom fusion | bytes 1064960 | tf_op jit(solution)/shard_map/jit(_take)/gather | solution.py:103
  332.7 4.3 %broadcast_select_fusion.1 = bf16[4096,64]{1,0:T(8,128)(2,1)} fusion(bf16[4096,64]{1,0:T(8,128)(2,1)} %gather_fusion.3, pred[4096]{0:T(1024)(128)(4,1)S(1)} %compare_and_fusion.1), kind=kLoop, calls=%fused_computation.65 | loop fusion | flops 262144 | bytes 1052672 | tf_op jit(solution)/shard_map/jit(_take)/select_n | solution.py:103
  338.5 16.7 %all_to_all.19 = bf16[16,256,64]{1,2,0:T(8,128)(2,1)S(1)} all-to-all(bf16[16,256,64]{1,2,0:T(8,128)(2,1)S(1)} %copy.21), channel_id=1, replica_groups=mesh['node'=16,'head'=16] {'head'}, dimensions={0} | all-to-all | bytes 1048576 | tf_op jit(solution)/shard_map/all_to_all | solution.py:104
  357.3 7.5 %fusion.32 = bf16[256,1024]{1,0:T(8,128)(2,1)} fusion(f32[256,1024]{1,0:T(8,128)} %copy-done.4, bf16[2048,1024]{1,0:T(8,128)(2,1)} %param.19, bf16[1024,2048]{1,0:T(8,128)(2,1)} %param.18, f32[1024]{0:T(1024)S(1)} %copy-done.14, f32[256]{0:T(256)S(1)} %add_rsqrt_fusion, f32[256]{0:T(256)S(1)} %broadcast_multiply_fusion), kind=kOutput, calls=%fused_computation.47 | convolution fusion | flops 2153775104 | bytes 9967616 | tf_op jit(solution)/shard_map/dot_general | solution.py:112
  (198 shorter events, 70.4 us)
Async XLA Ops:
  6.5 348.7 %copy-start = (bf16[1024,1024]{1,0:T(8,128)(2,1)S(1)}, bf16[1024,1024]{1,0:T(8,128)(2,1)}, u32[]{:S(2)}) copy-start(bf16[1024,1024]{1,0:T(8,128)(2,1)} %param.16) | copy-start | bytes 6291460
  6.5 82.7 %slice-start = ((bf16[1024,1,192]{0,2,1:T(8,128)(2,1)}), bf16[1024,1,64]{0,2,1:T(8,128)(2,1)S(1)}, s32[]{:S(2)}) async-start(bf16[1024,1,192]{0,2,1:T(8,128)(2,1)} %param.15), calls=%async_computation.2 | async-start | bytes 262144 | tf_op jit(solution)/shard_map/slice | solution.py:45
  6.5 82.7 %slice-start.1 = ((bf16[1024,1,192]{0,2,1:T(8,128)(2,1)}), bf16[1024,1,128]{0,2,1:T(8,128)(2,1)S(1)}, s32[]{:S(2)}) async-start(bf16[1024,1,192]{0,2,1:T(8,128)(2,1)} %param.15), calls=%async_computation.3 | async-start | bytes 524288 | tf_op jit(solution)/shard_map/slice | solution.py:45
  6.5 4.9 %copy-start.12 = (s32[1,4096]{1,0:T(1,128)S(1)}, s32[1,4096]{1,0:T(1,128)}, u32[]{:S(2)}) copy-start(s32[1,4096]{1,0:T(1,128)} %param.21) | copy-start | bytes 49156
  6.5 82.7 %all-gather.2.cloned.1.call-start = ((), (), s32[]{:S(2)}) async-start(), calls=%async_computation.1 | async-start | bytes 8912896 | tf_op jit(solution)/shard_map/all_gather | solution.py:48
  95.6 1.1 copy-start.5
  114.4 60.2 %copy-start.13 = (s32[32,8]{0,1:T(8,128)S(1)}, s32[32,8]{0,1:T(8,128)}, u32[]{:S(2)}) copy-start(s32[32,8]{0,1:T(8,128)} %param.20) | copy-start | bytes 3076
  117.8 26.0 %collective-permute-start = (bf16[4096,128]{1,0:T(8,128)(2,1)S(1)}, bf16[4096,128]{1,0:T(8,128)(2,1)S(1)}, u32[]{:S(2)}, u32[]{:S(2)}) collective-permute-start(bf16[4096,128]{1,0:T(8,128)(2,1)S(1)} %broadcast_select_fusion.3), channel_id=1, source_target_pairs={{0,224},{16,240},{32,0},{48,16},{64,32},{80,48},{96,64},{112,80},{... | collective-permute-start | bytes 3145736 | tf_op jit(solution)/shard_map/ppermute | solution.py:17
  143.8 1.0 copy-start.6
  144.8 14.2 %collective-permute-start.1 = (bf16[4096,128]{1,0:T(8,128)(2,1)S(1)}, bf16[4096,128]{1,0:T(8,128)(2,1)S(1)}, u32[]{:S(2)}, u32[]{:S(2)}) collective-permute-start(bf16[4096,128]{1,0:T(8,128)(2,1)S(1)} %collective-permute-done), channel_id=1, source_target_pairs={{0,16},{16,32},{32,48},{48,64},{64,80},{80,96},{96,112},{112,128},... | collective-permute-start | bytes 3145736 | tf_op jit(solution)/shard_map/ppermute | solution.py:17
  159.0 1.0 copy-start.8
  160.0 14.2 %collective-permute-start.2 = (bf16[4096,128]{1,0:T(8,128)(2,1)S(1)}, bf16[4096,128]{1,0:T(8,128)(2,1)S(1)}, u32[]{:S(2)}, u32[]{:S(2)}) collective-permute-start(bf16[4096,128]{1,0:T(8,128)(2,1)S(1)} %collective-permute-done.1), channel_id=1, source_target_pairs={{0,16},{16,32},{32,48},{48,64},{64,80},{80,96},{96,112},{112,128},... | collective-permute-start | bytes 3145736 | tf_op jit(solution)/shard_map/ppermute | solution.py:17
  174.2 20.0 %copy-start.10 = (bf16[4096,128]{1,0:T(8,128)(2,1)}, bf16[4096,128]{1,0:T(8,128)(2,1)S(1)}, u32[]{:S(2)}) copy-start(bf16[4096,128]{1,0:T(8,128)(2,1)S(1)} %collective-permute-done.2) | copy-start | bytes 3145732
  174.2 16.3 %collective-permute-start.3 = (bf16[4096,128]{1,0:T(8,128)(2,1)S(1)}, bf16[4096,128]{1,0:T(8,128)(2,1)}, u32[]{:S(2)}, u32[]{:S(2)}) collective-permute-start(bf16[4096,128]{1,0:T(8,128)(2,1)S(1)} %collective-permute-done.2), channel_id=1, source_target_pairs={{0,16},{16,32},{32,48},{48,64},{64,80},{80,96},{96,112},{112,128},... | collective-permute-start | bytes 3145736 | tf_op jit(solution)/shard_map/ppermute | solution.py:17
  190.5 26.6 %collective-permute-start.4 = (bf16[4096,128]{1,0:T(8,128)(2,1)}, bf16[4096,128]{1,0:T(8,128)(2,1)}, u32[]{:S(2)}, u32[]{:S(2)}) collective-permute-start(bf16[4096,128]{1,0:T(8,128)(2,1)} %collective-permute-done.3), channel_id=1, source_target_pairs={{0,16},{16,32},{32,48},{48,64},{64,80},{80,96},{96,112},{112,128},... | collective-permute-start | bytes 3145736 | tf_op jit(solution)/shard_map/ppermute | solution.py:17
  217.1 2.9 copy-start.11
  218.5 1.6 copy-start.9
  220.0 1.3 copy-start.7
  221.4 2.3 copy-start.3
  231.5 2.0 copy-start.1
  243.1 2.0 copy-start.1
  254.6 2.0 copy-start.1
  266.2 2.0 copy-start.1
  277.8 2.0 copy-start.1
  289.3 2.0 copy-start.1
  300.9 2.0 copy-start.1
  312.4 2.0 copy-start.1
  332.7 22.6 %copy-start.2 = (bf16[256,1024]{1,0:T(8,128)(2,1)S(1)}, bf16[256,1024]{1,0:T(8,128)(2,1)}, u32[]{:S(2)}) copy-start(bf16[256,1024]{1,0:T(8,128)(2,1)} %param.13) | copy-start | bytes 1572868
  355.2 2.1 copy-start.14
  356.1 1.0 copy-start.4
Sparse Core Ops, SparseCore 0:
  11.6 77.6 all-gather.1
where the time goes:
time: 373 us; the launch traced here: 372 us
  local copies, waits for them, and re-layouts  141 us (38%)
  waiting for transfers between devices  132 us (35%)
  matrix products  38.1 us (10%)
  other arithmetic  25.3 us (7%)
  blocking collectives  16.7 us (4%)
  between operations  13.6 us (4%)
  starting transfers between devices  4.69 us (1%)
    all_gather x1, waiting for transfers between devices, shards(): lax.all_gather(normed, 'head', axis=0, tiled=True)  77.8 us
    ppermute x5, waiting for transfers between devices, passed_along(): return lax.ppermute(x, axis, [(i, (i + by) % size) for i in range(size)])  53.9 us
    gather x16, local copies, waits for them, and re-layouts, attend(): picked = jnp.take(window_tiles, columns.reshape(tile_group * NNZ), axis=0)  45.3 us
    all_to_all x1, blocking collectives, shards(): lax.all_to_all(restored, 'head', split_axis=0, concat_axis=1, tiled=True)  16.7 us
    sub x8, matrix products, attend(): expd = jnp.exp(scores - row_max)  15.7 us
    scatter x1, local copies, waits for them, and re-layouts, shards(): inverse_order = jnp.zeros((rows_part,), jnp.int32).at[partition_permutati...  15.7 us
    gather x1, local copies, waits for them, and re-layouts, shards(): keyval = jnp.take(keyval_rows, partition_permutation, axis=0)  15 us
    gather x1, local copies, waits for them, and re-layouts, shards(): restored = jnp.take(attended, inverse_order, axis=0)  15 us
  transfers between devices with their start and end apart: 6, of which 4 were waited for; matrix products, arithmetic and copies ran while one was open for 10% of the time, Pallas kernels for 0%

commit v1 on v0

v1 whole, which is shorter than its diff:
```python
import math

import jax
import jax.numpy as jnp
from jax import lax
from jax.experimental import pallas as pl
from jax.experimental.pallas import tpu as pltpu
from jax.sharding import PartitionSpec as P

D = 1024
HD = 64
TILE = 128
NNZ = 8
REACH = 2
WINDOW = 2 * REACH + 1
UNROLL = 16


def passed_along(x, axis, by):
    size = lax.axis_size(axis)
    return lax.ppermute(x, axis, [(i, (i + by) % size) for i in range(size)])


def layer_norm(values, gain):
    row_mean = jnp.mean(values, -1, keepdims=True)
    centred = values - row_mean
    variance = jnp.mean(centred * centred, -1, keepdims=True)
    return centred * lax.rsqrt(variance + 1e-05) * gain


def reorder_kernel(order_ref, rows_ref, keyval_ref, query_ref, src_kv, src_q, dst_kv, dst_q):
    rows = rows_ref.shape[0]

    @pl.loop(0, rows // 128)
    def _(b):
        at = pl.ds(pl.multiple_of(b * 128, 128), 128)
        src_kv[at, :] = rows_ref[at, :128].astype(jnp.float32)
        src_q[at, :] = rows_ref[at, 128:].astype(jnp.float32)

    @pl.loop(0, rows // UNROLL)
    def _(b):
        base = pl.multiple_of(b * UNROLL, UNROLL)
        for r in range(UNROLL):
            at = order_ref[base + r]
            dst_kv[pl.ds(base + r, 1), :] = src_kv[pl.ds(at, 1), :]
            dst_q[pl.ds(base + r, 1), :] = src_q[pl.ds(at, 1), :]

    @pl.loop(0, rows // 128)
    def _(b):
        at = pl.ds(pl.multiple_of(b * 128, 128), 128)
        keyval_ref[at, :] = dst_kv[at, :].astype(jnp.bfloat16)
        query_ref[at, :] = dst_q[at, :].astype(jnp.bfloat16)


def reorder(order, rows):
    n = rows.shape[0]
    vmem = pl.BlockSpec(memory_space=pltpu.VMEM)
    return pl.pallas_call(
        reorder_kernel,
        out_shape=[jax.ShapeDtypeStruct((n, 2 * HD), jnp.bfloat16)] * 2,
        in_specs=[pl.BlockSpec(memory_space=pltpu.SMEM), vmem],
        out_specs=[vmem, vmem],
        scratch_shapes=[pltpu.VMEM((n, 2 * HD), jnp.float32)] * 4,
        compiler_params=pltpu.CompilerParams(vmem_limit_bytes=40 << 20),
        name="reorder",
    )(order, rows)


def attend_tile(t, position_ref, order_ref, query_ref, window, tile_out, restored):
    scale = math.log2(math.e) / math.sqrt(HD)
    query = query_ref[pl.ds(pl.multiple_of(t * TILE, TILE), TILE), :]
    keyval = jnp.concatenate([window[position_ref[t, n]] for n in range(NNZ)], axis=0)
    scores = lax.dot_general(
        query, keyval, (((1,), (1,)), ((), ())), preferred_element_type=jnp.float32
    )
    scores = scores * scale
    expd = jnp.exp2(scores - jnp.max(scores, -1, keepdims=True))
    total = jnp.sum(expd, -1, keepdims=True)
    mixed = jnp.dot(expd.astype(jnp.bfloat16), keyval, preferred_element_type=jnp.float32)
    tile_out[...] = mixed / total
    for r in range(TILE):
        restored[pl.ds(order_ref[t * TILE + r], 1), :] = tile_out[pl.ds(r, 1), :]


def attention_kernel(
    position_ref, order_ref, query_ref, b0, b1, b2, b3, b4, out_ref, window, tile_out, restored, sems
):
    tiles = query_ref.shape[0] // TILE
    copies = []
    for k, block in enumerate((b0, b1, b2, b3, b4)):
        copy = pltpu.make_async_copy(block, window.at[pl.ds(k * tiles, tiles)], sems.at[k])
        copy.start()
        copies.append(copy)
    for copy in copies:
        copy.wait()

    @pl.loop(0, tiles)
    def _(t):
        attend_tile(t, position_ref, order_ref, query_ref, window, tile_out, restored)

    @pl.loop(0, tiles)
    def _(t):
        at = pl.ds(pl.multiple_of(t * TILE, TILE), TILE)
        out_ref[at, :] = restored[at, HD:].astype(jnp.bfloat16)


def attention(position, order, query, blocks):
    n = query.shape[0]
    tiles = n // TILE
    smem = pl.BlockSpec(memory_space=pltpu.SMEM)
    vmem = pl.BlockSpec(memory_space=pltpu.VMEM)
    hbm = pl.BlockSpec(memory_space=pl.ANY)
    return pl.pallas_call(
        attention_kernel,
        out_shape=jax.ShapeDtypeStruct((n, HD), jnp.bfloat16),
        in_specs=[smem, smem, vmem] + [hbm] * WINDOW,
        out_specs=vmem,
        scratch_shapes=[
            pltpu.VMEM((WINDOW * tiles, TILE, 2 * HD), jnp.bfloat16),
            pltpu.VMEM((TILE, 2 * HD), jnp.float32),
            pltpu.VMEM((n, 2 * HD), jnp.float32),
            pltpu.SemaphoreType.DMA((WINDOW,)),
        ],
        compiler_params=pltpu.CompilerParams(vmem_limit_bytes=40 << 20),
        name="attention",
    )(position, order, query, *[b.reshape(tiles, TILE, 2 * HD) for b in blocks])


def shards(
    features,
    attn_gain,
    qkv_weight,
    out_weight,
    feedforward_norm_gain,
    up_weight,
    down_weight,
    tile_pattern,
    node_order,
):
    own_rows = features.shape[0]
    partitions = lax.axis_size("node")
    rows_part = own_rows * lax.axis_size("head")
    query_tiles = rows_part // TILE
    normed = layer_norm(features.astype(jnp.float32), attn_gain).astype(jnp.bfloat16)
    weight = qkv_weight[:, 0]
    weight = jnp.concatenate(
        [weight[:, HD:], weight[:, :HD], jnp.zeros((D, HD), jnp.bfloat16)], -1
    )
    projected = jnp.dot(
        lax.all_gather(normed, "head", axis=0, tiled=True),
        weight,
        preferred_element_type=jnp.float32,
    ).astype(jnp.bfloat16)
    order = node_order[0]
    keyval, query = reorder(order, projected)
    blocks = [
        keyval if by == 0 else passed_along(keyval, "node", -by)
        for by in range(-REACH, REACH + 1)
    ]
    partition = lax.axis_index("node")
    position = (
        tile_pattern // query_tiles - partition + REACH + partitions
    ) % partitions * query_tiles + tile_pattern % query_tiles
    restored = attention(position, order, query, blocks)
    gathered_heads = lax.all_to_all(restored, "head", split_axis=0, concat_axis=1, tiled=True)
    residual = features.astype(jnp.float32) + jnp.dot(
        gathered_heads, out_weight, preferred_element_type=jnp.float32
    )
    mlp_input = layer_norm(residual, feedforward_norm_gain).astype(jnp.bfloat16)
    hidden = jax.nn.gelu(jnp.dot(mlp_input, up_weight, preferred_element_type=jnp.float32)).astype(
        jnp.bfloat16
    )
    return (residual + jnp.dot(hidden, down_weight, preferred_element_type=jnp.float32)).astype(
        jnp.bfloat16
    )


def solution(mesh):
    return jax.shard_map(
        shards,
        mesh=mesh,
        in_specs=(
            P(("node", "head"), None),
            P(),
            P(None, "head", None),
            P(),
            P(),
            P(),
            P(),
            P("node", None),
            P("node", None),
        ),
        out_specs=P(("node", "head"), None),
        check_vma=False,
    )
```

time: 373 us -> 205 us (0.55)
  local copies, waits for them, and re-layouts: 141 us -> 5.75 us
  Pallas kernels: 0 us -> 32.3 us
  matrix products: 38.1 us -> 14.7 us
  other arithmetic: 25.3 us -> 5.11 us
  waiting for transfers between devices: 132 us -> 113 us
    gather x19 -> x0, local copies, waits for them, and re-layouts: 90.3 us -> none  [the longest x16 45.3 us: attend(): picked = jnp.take(window_tiles, columns.reshape(tile_group * NNZ), axis=0)]
    pallas_call x0 -> x2, Pallas kernels: none -> 32.3 us  [the longest x1 24.9 us: attention(): pl.pallas_call(attention_kernel, out_shape=jax.ShapeDtypeStruct((n, HD),...]
    select_n x20 -> x0, other arithmetic: 20 us -> none  [the longest x16 9.01 us: attend(): picked = jnp.take(window_tiles, columns.reshape(tile_group * NNZ), axis=0)]
    ppermute x5 -> x4, waiting for transfers between devices: 53.9 us -> 35.5 us  [passed_along(): return lax.ppermute(x, axis, [(i, (i + by) % size) for i in range(size)])]
    sub x8 -> x0, matrix products: 15.7 us -> none  [attend(): expd = jnp.exp(scores - row_max)]
    scatter x1 -> x0, local copies, waits for them, and re-layouts: 15.7 us -> none  [shards(): inverse_order = jnp.zeros((rows_part,), jnp.int32).at[partition_permutati...]
    dot_general x9 -> x1, matrix products: 14.1 us -> 5.85 us  [shards(): jnp.dot(lax.all_gather(normed, 'head', axis=0, tiled=True), weight, prefe...]
    dynamic_slice x8 -> x0, local copies, waits for them, and re-layouts: 6.81 us -> none  [shards(): lax.map(attend, (grouped_queries, grouped_slots))]
  transfers between devices with their start and end apart: 6 -> 5, of which waited for: 4 -> 4; matrix products, arithmetic and copies ran while one was open for 10% -> 0% of each run, Pallas kernels for 0% -> 0%
where the time goes in v1:
time: 205 us; the launch traced here: 204 us
  waiting for transfers between devices  113 us (55%)
  Pallas kernels  32.3 us (16%)
  blocking collectives  15.3 us (7%)
  matrix products  14.7 us (7%)
  between operations  13.5 us (7%)
  local copies, waits for them, and re-layouts  5.75 us (3%)
  other arithmetic  5.11 us (2%)
  starting transfers between devices  4.51 us (2%)
    all_gather x1, waiting for transfers between devices, shards(): lax.all_gather(normed, 'head', axis=0, tiled=True)  77.7 us
    ppermute x4, waiting for transfers between devices, passed_along(): return lax.ppermute(x, axis, [(i, (i + by) % size) for i in range(size)])  35.5 us
    pallas_call x1, Pallas kernels, attention(): pl.pallas_call(attention_kernel, out_shape=jax.ShapeDtypeStruct((n, HD),...  24.9 us
    all_to_all x1, blocking collectives, shards(): lax.all_to_all(restored, 'head', split_axis=0, concat_axis=1, tiled=True)  15.3 us
    pallas_call x1, Pallas kernels, reorder(): pl.pallas_call(reorder_kernel, out_shape=[jax.ShapeDtypeStruct((n, 2 * HD...  7.4 us
    dot_general x1, matrix products, shards(): jnp.dot(hidden, down_weight, preferred_element_type=jnp.float32)  6.94 us
    dot_general x1, matrix products, shards(): jnp.dot(lax.all_gather(normed, 'head', axis=0, tiled=True), weight, prefe...  5.85 us
    ppermute x4, starting transfers between devices, passed_along(): return lax.ppermute(x, axis, [(i, (i + by) % size) for i in range(size)])  4.51 us
  transfers between devices with their start and end apart: 5, of which 4 were waited for; matrix products, arithmetic and copies ran while one was open for 0% of the time, Pallas kernels for 0%

profile of v1, /device:TPU:96, one launch (start us, length us, event | category | flops | bytes accessed | tf_op | source)
XLA Modules:
  0.0 204.4 jit_solution(1782432587510223340)
XLA Ops:
  6.5 0.0 copy-start
  6.5 0.0 all-gather.2.cloned.1.call-start
  6.5 1.3 convert_reduce_fusion
  7.9 1.3 fusion.11
  9.2 2.1 %fusion.13 = bf16[256,1024]{1,0:T(8,128)(2,1)} fusion(bf16[256,1024]{1,0:T(8,128)(2,1)} %param.9, f32[1024]{0:T(1024)} %param.10, f32[256]{0:T(256)S(1)} %add_rsqrt_fusion.1, f32[256]{0:T(256)S(1)} %broadcast_multiply_fusion.1), kind=kLoop, calls=%fused_computation.19 | loop fusion | flops 1310720 | bytes 1054720 | tf_op jit(solution)/shard_map/convert_element_type | solution.py:144
  11.4 0.0 all-gather.2.cloned.1.call-update
  11.4 0.0 copy-done.6
  11.5 0.1 pad.2.clone
  11.5 77.7 %all-gather.2.cloned.1.call-done = bf16[4096,1024]{1,0:T(8,128)(2,1)} async-done(((bf16[256,1024]{1,0:T(8,128)(2,1)}), bf16[4096,1024]{1,0:T(8,128)(2,1)}) %all-gather.2.cloned.1.call-update) | async-done | bytes 8388624 | tf_op jit(solution)/shard_map/all_gather | solution.py:150
  89.2 5.8 %convolution_convert_fusion.rows_ref = bf16[4096,256]{1,0:T(8,128)(2,1)S(1)} fusion(bf16[4096,1024]{1,0:T(8,128)(2,1)} %all-gather.2.cloned.1.call-done, bf16[1024,64]{0,1:T(8,128)(2,1)S(1)} %slice.9, bf16[1024,128]{0,1:T(8,128)(2,1)S(1)} %slice.8, bf16[256]{0:T(256)(128)(2,1)S(1)} %pad.2.clone), kind=kOutput, calls=%fused_computation | convolution fusion | flops 2150105088 | bytes 10879488 | tf_op jit(solution)/shard_map/dot_general | solution.py:149
  95.1 0.0 copy-start.7
  95.1 7.4 %reorder.1 = (bf16[4096,128]{1,0:T(8,128)(2,1)S(1)}, bf16[4096,128]{1,0:T(8,128)(2,1)S(1)}) custom-call(s32[4096]{0:T(1024)S(1)} %bitcast.18, bf16[4096,256]{1,0:T(8,128)(2,1)S(1)} %convolution_convert_fusion.rows_ref), custom_call_target="tpu_custom_call" | custom-call | tf_op jit(solution)/shard_map/reorder/pallas_call | solution.py:58
  102.5 1.0 copy-done.3
  103.5 2.8 %collective-permute-start = (bf16[4096,128]{1,0:T(8,128)(2,1)S(1)}, bf16[4096,128]{1,0:T(8,128)(2,1)}, u32[]{:S(2)}, u32[]{:S(2)}) collective-permute-start(bf16[4096,128]{1,0:T(8,128)(2,1)S(1)} %get-tuple-element.8), channel_id=1, source_target_pairs={{0,32},{16,48},{32,64},{48,80},{64,96},{80,112},{96,128},{112,144}... | collective-permute-start | bytes 3145736 | tf_op jit(solution)/shard_map/ppermute | solution.py:21
  106.3 0.0 collective-permute-start.1
  106.3 1.7 collective-permute-start.2
  108.0 0.0 collective-permute-start.3
  108.0 1.0 copy-done.1
  109.0 0.1 copy.14
  109.1 20.7 %collective-permute-done = bf16[4096,128]{1,0:T(8,128)(2,1)} collective-permute-done((bf16[4096,128]{1,0:T(8,128)(2,1)S(1)}, bf16[4096,128]{1,0:T(8,128)(2,1)}, u32[]{:S(2)}, u32[]{:S(2)}) %collective-permute-start) | collective-permute-done | bytes 1048608 | tf_op jit(solution)/shard_map/ppermute | solution.py:21
  129.8 9.8 %collective-permute-done.1 = bf16[4096,128]{1,0:T(8,128)(2,1)} collective-permute-done((bf16[4096,128]{1,0:T(8,128)(2,1)S(1)}, bf16[4096,128]{1,0:T(8,128)(2,1)}, u32[]{:S(2)}, u32[]{:S(2)}) %collective-permute-start.1) | collective-permute-done | bytes 1048608 | tf_op jit(solution)/shard_map/ppermute | solution.py:21
  139.6 0.0 collective-permute-done.2
  139.6 5.1 %collective-permute-done.3 = bf16[4096,128]{1,0:T(8,128)(2,1)} collective-permute-done((bf16[4096,128]{1,0:T(8,128)(2,1)S(1)}, bf16[4096,128]{1,0:T(8,128)(2,1)}, u32[]{:S(2)}, u32[]{:S(2)}) %collective-permute-start.3) | collective-permute-done | bytes 1048608 | tf_op jit(solution)/shard_map/ppermute | solution.py:21
  144.7 1.2 copy-done.2
  145.9 1.2 copy-done.4
  147.1 24.9 %attention.1 = bf16[4096,64]{1,0:T(8,128)(2,1)S(1)} custom-call(s32[32,8]{1,0:T(8,128)S(1)} %fusion.35.position_ref, s32[4096]{0:T(1024)S(1)} %bitcast.19, bf16[4096,128]{1,0:T(8,128)(2,1)S(1)} %copy-done.4, bf16[32,128,128]{2,1,0:T(8,128)(2,1)} %bitcast.2.b0, bf16[32,128,128]{2,1,0:T(8,128)(2,1)} %bitcast.3.b1, bf16[32,128,128]{2,1,0:T(8,128)(2,1)S(1)} %bitcast.17, ...), custom_call_target="tpu_custom_call" | custom-call | tf_op jit(solution)/shard_map/attention/pallas_call | solution.py:113
  172.0 1.1 copy.18
  173.1 15.3 %all_to_all.19 = bf16[16,256,64]{1,2,0:T(8,128)(2,1)S(1)} all-to-all(bf16[16,256,64]{1,2,0:T(8,128)(2,1)} %copy.18), channel_id=1, replica_groups=mesh['node'=16,'head'=16] {'head'}, dimensions={0} | all-to-all | bytes 1048576 | tf_op jit(solution)/shard_map/all_to_all | solution.py:165
  188.5 1.9 fusion.42
  190.3 0.3 multiply_reduce_fusion
  190.6 0.0 copy-done.8
  190.6 6.9 %fusion.8 = bf16[256,1024]{1,0:T(8,128)(2,1)} fusion(f32[256,1024]{1,0:T(8,128)S(1)} %get-tuple-element.10, bf16[2048,1024]{1,0:T(8,128)(2,1)} %param.15, bf16[1024,2048]{1,0:T(8,128)(2,1)} %param.14, f32[1024]{0:T(1024)S(1)} %copy-done.8, f32[256]{0:T(256)S(1)} %add_rsqrt_fusion, f32[256]{0:T(256)S(1)} %broadcast_multiply_fusion), kind=kOutput, calls=%fused_computation.14 | convolution fusion | flops 2153775104 | bytes 9967616 | tf_op jit(solution)/shard_map/dot_general | solution.py:173
  (18 shorter events, 0.1 us)
Async XLA Ops:
  6.5 181.9 %copy-start = (bf16[1024,1024]{1,0:T(8,128)(2,1)S(1)}, bf16[1024,1024]{1,0:T(8,128)(2,1)}, u32[]{:S(2)}) copy-start(bf16[1024,1024]{1,0:T(8,128)(2,1)} %param.12) | copy-start | bytes 6291460
  6.5 4.9 %copy-start.6 = (bf16[1024,1,192]{0,2,1:T(8,128)(2,1)S(1)}, bf16[1024,1,192]{0,2,1:T(8,128)(2,1)}, u32[]{:S(2)}) copy-start(bf16[1024,1,192]{0,2,1:T(8,128)(2,1)} %param.11) | copy-start | bytes 1179652
  6.5 82.7 %all-gather.2.cloned.1.call-start = ((), (), s32[]{:S(2)}) async-start(), calls=%async_computation.1 | async-start | bytes 8912896 | tf_op jit(solution)/shard_map/all_gather | solution.py:150
  11.5 83.6 %copy-start.5 = (s32[1,4096]{1,0:T(1,128)S(1)}, s32[1,4096]{1,0:T(1,128)}, u32[]{:S(2)}) copy-start(s32[1,4096]{1,0:T(1,128)} %param.17) | copy-start | bytes 49156
  95.1 13.9 %copy-start.7 = (s32[32,8]{0,1:T(8,128)S(1)}, s32[32,8]{0,1:T(8,128)}, u32[]{:S(2)}) copy-start(s32[32,8]{0,1:T(8,128)} %param.16) | copy-start | bytes 3076
  102.5 1.0 copy-start.3
  103.5 26.3 %collective-permute-start = (bf16[4096,128]{1,0:T(8,128)(2,1)S(1)}, bf16[4096,128]{1,0:T(8,128)(2,1)}, u32[]{:S(2)}, u32[]{:S(2)}) collective-permute-start(bf16[4096,128]{1,0:T(8,128)(2,1)S(1)} %get-tuple-element.8), channel_id=1, source_target_pairs={{0,32},{16,48},{32,64},{48,80},{64,96},{80,112},{96,128},{112,144}... | collective-permute-start | bytes 3145736 | tf_op jit(solution)/shard_map/ppermute | solution.py:21
  106.3 33.3 %collective-permute-start.1 = (bf16[4096,128]{1,0:T(8,128)(2,1)S(1)}, bf16[4096,128]{1,0:T(8,128)(2,1)}, u32[]{:S(2)}, u32[]{:S(2)}) collective-permute-start(bf16[4096,128]{1,0:T(8,128)(2,1)S(1)} %get-tuple-element.8), channel_id=1, source_target_pairs={{0,16},{16,32},{32,48},{48,64},{64,80},{80,96},{96,112},{112,128},... | collective-permute-start | bytes 3145736 | tf_op jit(solution)/shard_map/ppermute | solution.py:21
  106.3 33.3 %collective-permute-start.2 = (bf16[4096,128]{1,0:T(8,128)(2,1)S(1)}, bf16[4096,128]{1,0:T(8,128)(2,1)}, u32[]{:S(2)}, u32[]{:S(2)}) collective-permute-start(bf16[4096,128]{1,0:T(8,128)(2,1)S(1)} %get-tuple-element.8), channel_id=1, source_target_pairs={{0,240},{16,0},{32,16},{48,32},{64,48},{80,64},{96,80},{112,96},{1... | collective-permute-start | bytes 3145736 | tf_op jit(solution)/shard_map/ppermute | solution.py:21
  108.0 36.6 %collective-permute-start.3 = (bf16[4096,128]{1,0:T(8,128)(2,1)S(1)}, bf16[4096,128]{1,0:T(8,128)(2,1)}, u32[]{:S(2)}, u32[]{:S(2)}) collective-permute-start(bf16[4096,128]{1,0:T(8,128)(2,1)S(1)} %get-tuple-element.8), channel_id=1, source_target_pairs={{0,224},{16,240},{32,0},{48,16},{64,32},{80,48},{96,64},{112,80},{... | collective-permute-start | bytes 3145736 | tf_op jit(solution)/shard_map/ppermute | solution.py:21
  108.0 1.0 copy-start.1
  144.7 1.2 copy-start.2
  145.9 1.2 copy-start.4
  188.5 2.2 %copy-start.8 = (f32[1024]{0:T(1024)S(1)}, f32[1024]{0:T(1024)}, u32[]{:S(2)}) copy-start(f32[1024]{0:T(1024)} %param.13) | copy-start | bytes 12292
Sparse Core Ops, SparseCore 0:
  11.5 77.6 all-gather.1

commit v2 on v1

v2 whole, which is shorter than its diff:
```python
import math

import jax
import jax.numpy as jnp
from jax import lax
from jax.experimental import pallas as pl
from jax.experimental.pallas import tpu as pltpu
from jax.sharding import PartitionSpec as P

D = 1024
HD = 64
TILE = 128
NNZ = 8
REACH = 2
WINDOW = 2 * REACH + 1
HALF = 3 * HD // 2
UNROLL = 16
CHUNKS = 8
NEAR = (0, 3, 1, 2)


def layer_norm(values, gain):
    row_mean = jnp.mean(values, -1, keepdims=True)
    centred = values - row_mean
    variance = jnp.mean(centred * centred, -1, keepdims=True)
    return centred * lax.rsqrt(variance + 1e-05) * gain


def project_kernel(
    features_ref, gain_ref, weight_ref, recv_ref,
    weights, normed, outgoing,
    ring_send, ring_recv, swap_send, swap_recv, head_send, head_recv,
):
    heads = weights.shape[0]
    side = math.isqrt(heads)
    me = lax.axis_index("head")
    node = lax.axis_index("node")
    core = lax.rem(node, 2)
    partner = node + 1 - 2 * core
    x = me // side
    y = lax.rem(me, side)
    first = x + core * (y - x)
    second = y + core * (x - y)
    first_stride = side - (side - 1) * core
    second_stride = 1 + (side - 1) * core
    piece = HALF // 2

    def head_of(da, db):
        return (
            lax.rem(first + da % side, side) * first_stride
            + lax.rem(second + db % side, side) * second_stride
        )

    def ring(s, m):
        offset = (0, 0, -1, 0, 0, 1)[m]
        part = (0, 1, 0, 1, 0, 1)[m]
        step = 1 if m < 3 else -1
        if s == 0:
            block, target, own = head_of(offset, 0), head_of(step, 0), offset == 0
        else:
            across = NEAR[s - 1]
            block, target = head_of(across, offset), head_of(0, step)
            own = across == 0 and offset == 0
        there = weights.at[block, core, pl.ds(part * piece, piece)]
        here = weight_ref.at[core, pl.ds(part * piece, piece)] if own else there
        return pltpu.make_async_remote_copy(
            src_ref=here, dst_ref=there,
            send_sem=ring_send.at[s, m], recv_sem=ring_recv.at[s, m],
            device_id={"head": target}, device_id_type=pl.DeviceIdType.MESH,
        )

    def swap(da, db):
        ref = weights.at[head_of(da, db), core]
        slot = (da % side) * first_stride + (db % side) * second_stride
        return pltpu.make_async_remote_copy(
            src_ref=ref, dst_ref=ref, send_sem=swap_send.at[slot], recv_sem=swap_recv.at[slot],
            device_id={"node": partner}, device_id_type=pl.DeviceIdType.MESH,
        )

    def to_head(slot):
        target = lax.rem(x + slot // side, side) * side + lax.rem(y + slot % side, side)
        return pltpu.make_async_remote_copy(
            src_ref=outgoing.at[slot], dst_ref=recv_ref.at[me],
            send_sem=head_send.at[slot], recv_sem=head_recv.at[slot],
            device_id={"head": target}, device_id_type=pl.DeviceIdType.MESH,
        )

    barrier = pltpu.get_barrier_semaphore()
    for k in range(1, heads):
        peer = lax.rem(x + k // side, side) * side + lax.rem(y + k % side, side)
        pl.semaphore_signal(
            barrier, inc=1, device_id={"head": peer}, device_id_type=pl.DeviceIdType.MESH
        )
    pl.semaphore_signal(
        barrier, inc=1, device_id={"node": partner}, device_id_type=pl.DeviceIdType.MESH
    )
    pl.semaphore_wait(barrier, heads)

    def own_sends(s):
        for m in (0, 3, 1, 4):
            ring(s, m).start()

    own_sends(0)
    own_sends(1)

    @pl.loop(0, features_ref.shape[0] // 32)
    def _(i):
        at = pl.ds(pl.multiple_of(i * 32, 32), 32)
        rows = features_ref[at, :].astype(jnp.float32)
        normed[at, :] = layer_norm(rows, gain_ref[...]).astype(jnp.bfloat16)

    rows_half = features_ref.shape[0] // 2

    def project(weight, put):
        result = lax.dot_general(
            normed[...], weight.reshape(2 * HALF, D), (((1,), (1,)), ((), ())),
            preferred_element_type=jnp.float32,
        ).astype(jnp.bfloat16)
        put[: 2 * rows_half, :] = result[:, : 2 * HD]
        put[2 * rows_half :, :] = jnp.concatenate(
            [result[:rows_half, 2 * HD :], result[rows_half:, 2 * HD :]], axis=1
        )

    def project_head(dx, dy):
        slot = dx * side + dy
        block = lax.rem(x + dx, side) * side + lax.rem(y + dy, side)
        other = weights.at[block, 1 - core]
        pltpu.make_async_remote_copy(
            src_ref=other, dst_ref=other, send_sem=swap_send.at[slot], recv_sem=swap_recv.at[slot],
            device_id={"node": partner}, device_id_type=pl.DeviceIdType.MESH,
        ).wait_recv()
        project(weights[block], outgoing.at[slot])
        to_head(slot).start()

    project(weight_ref[...], recv_ref.at[me])

    def near(s):
        ring(s, 0).wait_recv()
        ring(s, 2).start()
        ring(s, 3).wait_recv()
        ring(s, 5).start()
        ring(s, 1).wait_recv()
        ring(s, 4).wait_recv()

    def far(s):
        ring(s, 2).wait_recv()
        ring(s, 5).wait_recv()

    near(0)
    own_sends(2)
    own_sends(3)
    swap(-1, 0).start()
    swap(1, 0).start()
    near(1)
    swap(0, -1).start()
    swap(0, 1).start()
    far(0)
    own_sends(4)
    swap(2, 0).start()
    far(1)
    swap(0, 2).start()

    @pl.loop(0, 4)
    def _(i):
        long = 1 + 2 * lax.rem(i, 2)
        project_head((1 - i // 2) * long, (i // 2) * long)

    near(2)
    swap(-1, -1).start()
    swap(-1, 1).start()
    near(3)
    swap(1, -1).start()
    swap(1, 1).start()

    @pl.loop(0, 2)
    def _(i):
        project_head(2 * (1 - i), 2 * i)

    far(2)
    swap(-1, 2).start()
    far(3)
    swap(1, 2).start()
    near(4)
    swap(2, -1).start()
    swap(2, 1).start()

    @pl.loop(0, 4)
    def _(i):
        project_head(1 + 2 * lax.rem(i, 2), 1 + 2 * (i // 2))

    far(4)
    swap(2, 2).start()

    @pl.loop(0, 4)
    def _(i):
        long = 1 + 2 * lax.rem(i, 2)
        group = i // 2
        project_head((1 - group) * long + 2 * group, 2 * (1 - group) + group * long)

    project_head(2, 2)

    for s in range(5):
        for m in range(6):
            ring(s, m).wait_send()
    for da in range(side):
        for db in range(side):
            if da or db:
                swap(da, db).wait_send()
    for slot in range(1, heads):
        to_head(slot).wait_send()
        to_head(slot).wait_recv()


def project(features, gain, weight):
    heads = lax.axis_size("head")
    rows = features.shape[0]
    vmem = pl.BlockSpec(memory_space=pltpu.VMEM)
    dma = pltpu.SemaphoreType.DMA
    return pl.pallas_call(
        project_kernel,
        out_shape=jax.ShapeDtypeStruct((heads, rows * 3 // 2, 2 * HD), jnp.bfloat16),
        in_specs=[vmem] * 3,
        out_specs=vmem,
        scratch_shapes=[
            pltpu.VMEM((heads, 2, HALF, D), jnp.bfloat16),
            pltpu.VMEM((rows, D), jnp.bfloat16),
            pltpu.VMEM((heads, rows * 3 // 2, 2 * HD), jnp.bfloat16),
            dma((5, 6)),
            dma((5, 6)),
            dma((heads,)),
            dma((heads,)),
            dma((heads,)),
            dma((heads,)),
        ],
        compiler_params=pltpu.CompilerParams(
            collective_id=0, has_side_effects=True, vmem_limit_bytes=40 << 20
        ),
        name="project",
    )(features, gain.reshape(1, D), weight)


def exchange_kernel(
    order_ref, rows_ref, window_ref, query_ref,
    source, reordered, send, recv,
):
    heads = rows_ref.shape[0]
    owned = rows_ref.shape[1] * 2 // 3
    rows = heads * owned
    size = lax.axis_size("node")
    tiles = rows // TILE
    per_chunk = tiles // CHUNKS
    chunk_rows = rows // CHUNKS
    node = lax.axis_index("node")
    core = lax.rem(node, 2)
    partner = node + 1 - 2 * core
    above = lax.rem(node + 2, size)
    below = lax.rem(node + size - 2, size)

    barrier = pltpu.get_barrier_semaphore()
    for peer in (above, below, partner):
        pl.semaphore_signal(
            barrier, inc=1, device_id={"node": peer}, device_id_type=pl.DeviceIdType.MESH
        )

    def flow(f, i):
        source_slot = (REACH, REACH, REACH, 4 - 4 * core)[f]
        target_slot = (0, 2 * REACH, 1 + 2 * core, 3 - 2 * core)[f]
        at = pl.ds(i * per_chunk, per_chunk)
        return pltpu.make_async_remote_copy(
            src_ref=window_ref.at[source_slot, at], dst_ref=window_ref.at[target_slot, at],
            send_sem=send.at[f, i], recv_sem=recv.at[f, i],
            device_id={"node": (above, below, partner, partner)[f]},
            device_id_type=pl.DeviceIdType.MESH,
        )

    @pl.loop(0, heads)
    def _(j):
        at = pl.ds(pl.multiple_of(j * owned, owned), owned)
        source[at, :] = rows_ref[j, :owned].astype(jnp.float32)

    def pick(base):
        @pl.loop(0, chunk_rows // UNROLL)
        def _(b):
            start = pl.multiple_of(base + b * UNROLL, UNROLL)
            for r in range(UNROLL):
                reordered[pl.ds(start + r, 1), :] = source[pl.ds(order_ref[start + r], 1), :]

    pl.semaphore_wait(barrier, 3)

    @pl.loop(0, CHUNKS)
    def _(i):
        pick(i * chunk_rows)
        for k in range(per_chunk):
            tile = i * per_chunk + k
            at = pl.ds(pl.multiple_of(tile * TILE, TILE), TILE)
            window_ref[REACH, tile] = reordered[at, :].astype(jnp.bfloat16)

        @pl.when(i > 0)
        def _():
            for f in range(3):
                flow(f, i - 1).start()

    lane = lax.broadcasted_iota(jnp.int32, (owned // 2, 2 * HD), 1)

    @pl.loop(0, heads)
    def _(j):
        packed = rows_ref[j, owned:].astype(jnp.float32)
        at = pl.multiple_of(j * owned, owned)
        source[pl.ds(at, owned // 2), :] = jnp.where(lane < HD, packed, 0.0)
        source[pl.ds(at + owned // 2, owned // 2), :] = jnp.where(
            lane < HD, pltpu.roll(packed, HD, 1), 0.0
        )

    for f in range(3):
        flow(f, CHUNKS - 1).start()

    def took(f, i):
        at = pl.ds(i * per_chunk, per_chunk)
        pltpu.make_async_remote_copy(
            src_ref=window_ref.at[0, at], dst_ref=window_ref.at[0, at],
            send_sem=send.at[f, i], recv_sem=recv.at[f, i],
            device_id={"node": partner}, device_id_type=pl.DeviceIdType.MESH,
        ).wait_recv()

    @pl.loop(0, CHUNKS)
    def _(i):
        pick(i * chunk_rows)
        for k in range(per_chunk):
            at = pl.ds(pl.multiple_of((i * per_chunk + k) * TILE, TILE), TILE)
            query_ref[at, :] = reordered[at, :].astype(jnp.bfloat16)
        took(1 - core, i)
        flow(3, i).start()

    @pl.loop(0, CHUNKS)
    def _(i):
        took(core, i)
        took(2, i)
        took(3, i)
        for f in range(4):
            flow(f, i).wait_send()


def exchange(order, rows):
    heads = rows.shape[0]
    n = heads * rows.shape[1] * 2 // 3
    vmem = pl.BlockSpec(memory_space=pltpu.VMEM)
    return pl.pallas_call(
        exchange_kernel,
        out_shape=[
            jax.ShapeDtypeStruct((WINDOW, n // TILE, TILE, 2 * HD), jnp.bfloat16),
            jax.ShapeDtypeStruct((n, 2 * HD), jnp.bfloat16),
        ],
        in_specs=[pl.BlockSpec(memory_space=pltpu.SMEM), vmem],
        out_specs=[vmem, vmem],
        scratch_shapes=[
            pltpu.VMEM((n, 2 * HD), jnp.float32),
            pltpu.VMEM((n, 2 * HD), jnp.float32),
            pltpu.SemaphoreType.DMA((4, CHUNKS)),
            pltpu.SemaphoreType.DMA((4, CHUNKS)),
        ],
        compiler_params=pltpu.CompilerParams(
            collective_id=1, has_side_effects=True, vmem_limit_bytes=40 << 20
        ),
        name="exchange",
    )(order, rows)


def attend_tile(t, position_ref, order_ref, query_ref, window, tile_out, restored):
    scale = math.log2(math.e) / math.sqrt(HD)
    query = query_ref[pl.ds(pl.multiple_of(t * TILE, TILE), TILE), :]
    keyval = jnp.concatenate([window[position_ref[t, n]] for n in range(NNZ)], axis=0)
    scores = lax.dot_general(
        query, keyval, (((1,), (1,)), ((), ())), preferred_element_type=jnp.float32
    )
    scores = scores * scale
    expd = jnp.exp2(scores - jnp.max(scores, -1, keepdims=True))
    total = jnp.sum(expd, -1, keepdims=True)
    mixed = jnp.dot(expd.astype(jnp.bfloat16), keyval, preferred_element_type=jnp.float32)
    tile_out[...] = mixed / total
    for r in range(TILE):
        restored[pl.ds(order_ref[t * TILE + r], 1), :] = tile_out[pl.ds(r, 1), :]


def attention_kernel(
    position_ref, order_ref, query_ref, window, out_ref, tile_out, restored
):
    tiles = query_ref.shape[0] // TILE

    @pl.loop(0, tiles)
    def _(t):
        attend_tile(t, position_ref, order_ref, query_ref, window, tile_out, restored)

    @pl.loop(0, tiles)
    def _(t):
        at = pl.ds(pl.multiple_of(t * TILE, TILE), TILE)
        out_ref[at, :] = restored[at, HD:].astype(jnp.bfloat16)


def attention(position, order, query, window):
    n = query.shape[0]
    smem = pl.BlockSpec(memory_space=pltpu.SMEM)
    vmem = pl.BlockSpec(memory_space=pltpu.VMEM)
    return pl.pallas_call(
        attention_kernel,
        out_shape=jax.ShapeDtypeStruct((n, HD), jnp.bfloat16),
        in_specs=[smem, smem, vmem, vmem],
        out_specs=vmem,
        scratch_shapes=[
            pltpu.VMEM((TILE, 2 * HD), jnp.float32),
            pltpu.VMEM((n, 2 * HD), jnp.float32),
        ],
        compiler_params=pltpu.CompilerParams(vmem_limit_bytes=40 << 20),
        name="attention",
    )(position, order, query, window.reshape(WINDOW * n // TILE, TILE, 2 * HD))


def shards(
    features,
    attn_gain,
    qkv_weight,
    out_weight,
    feedforward_norm_gain,
    up_weight,
    down_weight,
    tile_pattern,
    node_order,
):
    own_rows = features.shape[0]
    partitions = lax.axis_size("node")
    rows_part = own_rows * lax.axis_size("head")
    query_tiles = rows_part // TILE
    weight = qkv_weight[:, 0].T
    weight = jnp.concatenate([weight[HD:], weight[:HD]], 0).reshape(2, HALF, D)
    order = node_order[0]
    window, query = exchange(order, project(features, attn_gain, weight))
    partition = lax.axis_index("node")
    position = (
        tile_pattern // query_tiles - partition + REACH + partitions
    ) % partitions * query_tiles + tile_pattern % query_tiles
    restored = attention(position, order, query, window)
    gathered_heads = lax.all_to_all(restored, "head", split_axis=0, concat_axis=1, tiled=True)
    residual = features.astype(jnp.float32) + jnp.dot(
        gathered_heads, out_weight, preferred_element_type=jnp.float32
    )
    mlp_input = layer_norm(residual, feedforward_norm_gain).astype(jnp.bfloat16)
    hidden = jax.nn.gelu(jnp.dot(mlp_input, up_weight, preferred_element_type=jnp.float32)).astype(
        jnp.bfloat16
    )
    return (residual + jnp.dot(hidden, down_weight, preferred_element_type=jnp.float32)).astype(
        jnp.bfloat16
    )


def solution(mesh):
    return jax.shard_map(
        shards,
        mesh=mesh,
        in_specs=(
            P(("node", "head"), None),
            P(),
            P(None, "head", None),
            P(),
            P(),
            P(),
            P(),
            P("node", None),
            P("node", None),
        ),
        out_specs=P(("node", "head"), None),
        check_vma=False,
    )
```

time: 205 us -> 137 us (0.67)
  waiting for transfers between devices: 113 us -> 0 us
  Pallas kernels: 32.3 us -> 103 us
  between operations: 13.5 us -> 0.08 us
  matrix products: 14.7 us -> 8.82 us
  other arithmetic: 5.11 us -> 0.32 us
  starting transfers between devices: 4.51 us -> 0 us
  blocking collectives: 15.3 us -> 17.9 us
    all_gather x1 -> x0, waiting for transfers between devices: 77.7 us -> none  [shards(): lax.all_gather(normed, 'head', axis=0, tiled=True)]
    pallas_call x1 -> x2, Pallas kernels: 7.4 us -> 80.1 us  [the longest x1 49.5 us: project(): pl.pallas_call(project_kernel, out_shape=jax.ShapeDtypeStruct((heads, row...]
    ppermute x4 -> x0, waiting for transfers between devices: 35.5 us -> none  [passed_along(): return lax.ppermute(x, axis, [(i, (i + by) % size) for i in range(size)])]
    dot_general x1 -> x0, matrix products: 5.85 us -> none  [shards(): jnp.dot(lax.all_gather(normed, 'head', axis=0, tiled=True), weight, prefe...]
    ppermute x4 -> x0, starting transfers between devices: 4.51 us -> none  [passed_along(): return lax.ppermute(x, axis, [(i, (i + by) % size) for i in range(size)])]
    all_to_all x1, blocking collectives: 15.3 us -> 17.9 us  [shards(): lax.all_to_all(restored, 'head', split_axis=0, concat_axis=1, tiled=True)]
    pallas_call x1, Pallas kernels: 24.9 us -> 22.7 us  [attention(): pl.pallas_call(attention_kernel, out_shape=jax.ShapeDtypeStruct((n, HD),...]
    convert_element_type x1 -> x0, other arithmetic: 2.14 us -> none  [shards(): layer_norm(features.astype(jnp.float32), attn_gain).astype(jnp.bfloat16)]
  transfers between devices with their start and end apart: 5 -> 0, of which waited for: 4 -> 0; matrix products, arithmetic and copies ran while one was open for 0% -> 0% of each run, Pallas kernels for 0% -> 0%
where the time goes in v2:
time: 137 us; the launch traced here: 136 us
  Pallas kernels  103 us (75%)
  blocking collectives  17.9 us (13%)
  matrix products  8.82 us (6%)
  local copies, waits for them, and re-layouts  5.68 us (4%)
    pallas_call x1, Pallas kernels, project(): pl.pallas_call(project_kernel, out_shape=jax.ShapeDtypeStruct((heads, row...  49.5 us
    pallas_call x1, Pallas kernels, exchange(): pl.pallas_call(exchange_kernel, out_shape=[jax.ShapeDtypeStruct((WINDOW,...  30.6 us
    pallas_call x1, Pallas kernels, attention(): pl.pallas_call(attention_kernel, out_shape=jax.ShapeDtypeStruct((n, HD),...  22.7 us
    all_to_all x1, blocking collectives, shards(): lax.all_to_all(restored, 'head', split_axis=0, concat_axis=1, tiled=True)  17.9 us
    dot_general x1, matrix products, shards(): jnp.dot(hidden, down_weight, preferred_element_type=jnp.float32)  6.94 us

profile of v2, /device:TPU:96, one launch (start us, length us, event | category | flops | bytes accessed | tf_op | source)
XLA Modules:
  0.0 135.6 jit_solution(14215069828247560901)
XLA Ops:
  0.0 0.0 copy-start
  0.0 0.0 copy-start.2
  0.0 1.1 slice.8
  1.1 0.9 slice.9
  2.1 0.8 copy.14
  2.9 0.0 copy-start.1
  2.9 1.0 copy-done.1
  3.9 0.0 copy-start.3
  3.9 0.7 copy-done.3
  4.6 49.5 %project.1.rows_ref = bf16[16,384,128]{2,1,0:T(8,128)(2,1)S(1)} custom-call(bf16[256,1024]{1,0:T(8,128)(2,1)S(1)} %copy-done.1, f32[1,1024]{1,0:T(1,128)S(1)} %bitcast.20, bf16[2,96,1024]{2,1,0:T(8,128)(2,1)S(1)} %bitcast.17), custom_call_target="tpu_custom_call" | custom-call | tf_op jit(solution)/shard_map/project/pallas_call | solution.py:219
  54.1 0.0 copy-done.2
  54.1 30.6 %exchange.1 = (bf16[5,32,128,128]{3,2,1,0:T(8,128)(2,1)S(1)}, bf16[4096,128]{1,0:T(8,128)(2,1)S(1)}) custom-call(s32[4096]{0:T(1024)S(1)} %bitcast.18, bf16[16,384,128]{2,1,0:T(8,128)(2,1)S(1)} %project.1.rows_ref), custom_call_target="tpu_custom_call" | custom-call | tf_op jit(solution)/shard_map/exchange/pallas_call | solution.py:347
  84.8 22.7 %attention.1 = bf16[4096,64]{1,0:T(8,128)(2,1)S(1)} custom-call(s32[32,8]{1,0:T(8,128)S(1)} %fusion.25.position_ref, s32[4096]{0:T(1024)S(1)} %bitcast.19, bf16[4096,128]{1,0:T(8,128)(2,1)S(1)} %get-tuple-element.7.query_ref, bf16[160,128,128]{2,1,0:T(8,128)(2,1)S(1)} %bitcast.15), custom_call_target="tpu_custom_call" | custom-call | tf_op jit(solution)/shard_map/attention/pallas_call | solution.py:403
  107.5 1.1 copy.18
  108.6 17.9 %all_to_all.19 = bf16[16,256,64]{1,2,0:T(8,128)(2,1)S(1)} all-to-all(bf16[16,256,64]{1,2,0:T(8,128)(2,1)} %copy.18), channel_id=1, replica_groups=mesh['node'=16,'head'=16] {'head'}, dimensions={0} | all-to-all | bytes 1048576 | tf_op jit(solution)/shard_map/all_to_all | solution.py:441
  126.5 0.0 copy-done
  126.5 0.0 copy-start.4
  126.5 1.9 %fusion.31 = (f32[256]{0:T(256)S(1)}, f32[256,1024]{1,0:T(8,128)S(1)}) fusion(bf16[256,1024]{0,1:T(8,128)(2,1)S(1)} %bitcast.21, bf16[1024,1024]{1,0:T(8,128)(2,1)S(1)} %copy-done, bf16[256,1024]{1,0:T(8,128)(2,1)} %features_ref.1), kind=kOutput, calls=%fused_computation.44 | convolution fusion | flops 537657088 | bytes 4195328 | tf_op jit(solution)/shard_map/dot_general | solution.py:442
  128.4 0.3 multiply_reduce_fusion
  128.6 0.0 copy-done.4
  128.7 6.9 %fusion.8 = bf16[256,1024]{1,0:T(8,128)(2,1)} fusion(f32[256,1024]{1,0:T(8,128)S(1)} %get-tuple-element.10, bf16[2048,1024]{1,0:T(8,128)(2,1)} %param.15, bf16[1024,2048]{1,0:T(8,128)(2,1)} %param.14, f32[1024]{0:T(1024)S(1)} %copy-done.4, f32[256]{0:T(256)S(1)} %add_rsqrt_fusion, f32[256]{0:T(256)S(1)} %broadcast_multiply_fusion), kind=kOutput, calls=%fused_computation.11 | convolution fusion | flops 2153775104 | bytes 9967616 | tf_op jit(solution)/shard_map/dot_general | solution.py:449
  (4 shorter events, 0.1 us)
Async XLA Ops:
  0.0 126.5 %copy-start = (bf16[1024,1024]{1,0:T(8,128)(2,1)S(1)}, bf16[1024,1024]{1,0:T(8,128)(2,1)}, u32[]{:S(2)}) copy-start(bf16[1024,1024]{1,0:T(8,128)(2,1)} %param.12) | copy-start | bytes 6291460
  0.0 54.1 %copy-start.2 = (s32[1,4096]{1,0:T(1,128)S(1)}, s32[1,4096]{1,0:T(1,128)}, u32[]{:S(2)}) copy-start(s32[1,4096]{1,0:T(1,128)} %param.17) | copy-start | bytes 49156
  2.9 1.0 copy-start.1
  3.9 0.7 copy-start.3
  126.5 2.2 %copy-start.4 = (f32[1024]{0:T(1024)S(1)}, f32[1024]{0:T(1024)}, u32[]{:S(2)}) copy-start(f32[1024]{0:T(1024)} %param.13) | copy-start | bytes 12292

commit v3 on v2

--- a/solution.py
+++ b/solution.py
@@ -17,6 +17,8 @@
 UNROLL = 16
 CHUNKS = 8
 NEAR = (0, 3, 1, 2)
+TOGETHER = 4
+FF_BLOCK = 512
 
 
 def layer_norm(values, gain):
@@ -112,8 +114,9 @@
     rows_half = features_ref.shape[0] // 2
 
     def project(weight, put):
+        weight = weight.reshape(2 * HALF, D)
         result = lax.dot_general(
-            normed[...], weight.reshape(2 * HALF, D), (((1,), (1,)), ((), ())),
+            normed[...], jnp.concatenate([weight[HD:], weight[:HD]], 0), (((1,), (1,)), ((), ())),
             preferred_element_type=jnp.float32,
         ).astype(jnp.bfloat16)
         put[: 2 * rows_half, :] = result[:, : 2 * HD]
@@ -233,7 +236,7 @@
             dma((heads,)),
         ],
         compiler_params=pltpu.CompilerParams(
-            collective_id=0, has_side_effects=True, vmem_limit_bytes=40 << 20
+            collective_id=0, has_side_effects=True, vmem_limit_bytes=67043328
         ),
         name="project",
     )(features, gain.reshape(1, D), weight)
@@ -359,59 +362,180 @@
             pltpu.SemaphoreType.DMA((4, CHUNKS)),
         ],
         compiler_params=pltpu.CompilerParams(
-            collective_id=1, has_side_effects=True, vmem_limit_bytes=40 << 20
+            collective_id=1, has_side_effects=True, vmem_limit_bytes=67043328
         ),
         name="exchange",
     )(order, rows)
 
 
-def attend_tile(t, position_ref, order_ref, query_ref, window, tile_out, restored):
+def attend(tiles, position_ref, order_ref, query_ref, window, tile_out, restored):
     scale = math.log2(math.e) / math.sqrt(HD)
-    query = query_ref[pl.ds(pl.multiple_of(t * TILE, TILE), TILE), :]
-    keyval = jnp.concatenate([window[position_ref[t, n]] for n in range(NNZ)], axis=0)
-    scores = lax.dot_general(
-        query, keyval, (((1,), (1,)), ((), ())), preferred_element_type=jnp.float32
-    )
-    scores = scores * scale
-    expd = jnp.exp2(scores - jnp.max(scores, -1, keepdims=True))
-    total = jnp.sum(expd, -1, keepdims=True)
-    mixed = jnp.dot(expd.astype(jnp.bfloat16), keyval, preferred_element_type=jnp.float32)
-    tile_out[...] = mixed / total
-    for r in range(TILE):
-        restored[pl.ds(order_ref[t * TILE + r], 1), :] = tile_out[pl.ds(r, 1), :]
+    keyvals, scores = [], []
+    for t in tiles:
+        query = query_ref[pl.ds(pl.multiple_of(t * TILE, TILE), TILE), :]
+        keyval = jnp.concatenate([window[position_ref[t, n]] for n in range(NNZ)], axis=0)
+        keyvals.append(keyval)
+        scores.append(
+            lax.dot_general(
+                query, keyval, (((1,), (1,)), ((), ())), preferred_element_type=jnp.float32
+            )
+        )
+    for k, t in enumerate(tiles):
+        scaled = scores[k] * scale
+        expd = jnp.exp2(scaled - jnp.max(scaled, -1, keepdims=True))
+        total = jnp.sum(expd, -1, keepdims=True)
+        mixed = jnp.dot(
+            expd.astype(jnp.bfloat16), keyvals[k], preferred_element_type=jnp.float32
+        )
+        tile_out[k] = mixed / total
+    for k, t in enumerate(tiles):
+        for r in range(TILE):
+            restored[pl.ds(order_ref[t * TILE + r], 1), :] = tile_out[k, pl.ds(r, 1), :]
 
 
 def attention_kernel(
     position_ref, order_ref, query_ref, window, out_ref, tile_out, restored
 ):
     tiles = query_ref.shape[0] // TILE
-
-    @pl.loop(0, tiles)
-    def _(t):
-        attend_tile(t, position_ref, order_ref, query_ref, window, tile_out, restored)
-
-    @pl.loop(0, tiles)
-    def _(t):
-        at = pl.ds(pl.multiple_of(t * TILE, TILE), TILE)
-        out_ref[at, :] = restored[at, HD:].astype(jnp.bfloat16)
-
-
-def attention(position, order, query, window):
+    heads, half = out_ref.shape[:2]
+
+    @pl.loop(0, tiles // TOGETHER)
+    def _(i):
+        attend(
+            [i * TOGETHER + k for k in range(TOGETHER)],
+            position_ref, order_ref, query_ref, window, tile_out, restored,
+        )
+
+    lane = lax.broadcasted_iota(jnp.int32, (half, 2 * HD), 1)
+
+    @pl.loop(0, heads)
+    def _(j):
+        at = pl.multiple_of(j * 2 * half, 2 * half)
+        low = pltpu.roll(restored[pl.ds(at, half), :], HD, 1)
+        high = restored[pl.ds(at + half, half), :]
+        out_ref[j] = jnp.where(lane < HD, low, high).astype(jnp.bfloat16)
+
+
+def attention(position, order, query, window, heads):
     n = query.shape[0]
     smem = pl.BlockSpec(memory_space=pltpu.SMEM)
     vmem = pl.BlockSpec(memory_space=pltpu.VMEM)
     return pl.pallas_call(
         attention_kernel,
-        out_shape=jax.ShapeDtypeStruct((n, HD), jnp.bfloat16),
+        out_shape=jax.ShapeDtypeStruct((heads, n // heads // 2, 2 * HD), jnp.bfloat16),
         in_specs=[smem, smem, vmem, vmem],
         out_specs=vmem,
         scratch_shapes=[
-            pltpu.VMEM((TILE, 2 * HD), jnp.float32),
+            pltpu.VMEM((TOGETHER, TILE, 2 * HD), jnp.float32),
             pltpu.VMEM((n, 2 * HD), jnp.float32),
         ],
-        compiler_params=pltpu.CompilerParams(vmem_limit_bytes=40 << 20),
+        compiler_params=pltpu.CompilerParams(vmem_limit_bytes=67043328),
         name="attention",
     )(position, order, query, window.reshape(WINDOW * n // TILE, TILE, 2 * HD))
+
+
+def finish_kernel(
+    attended_ref, features_ref, gain_ref, out_weight_ref, up_ref, down_ref, updated_ref,
+    out_weight, up, down, received, gathered, residual, normed,
+    load_sem, send, recv,
+):
+    heads, half = attended_ref.shape[:2]
+    side = math.isqrt(heads)
+    me = lax.axis_index("head")
+    x = me // side
+    y = lax.rem(me, side)
+    barrier = pltpu.get_barrier_semaphore()
+
+    def peer(slot):
+        return lax.rem(x + slot // side, side) * side + lax.rem(y + slot % side, side)
+
+    for slot in range(1, heads):
+        pl.semaphore_signal(
+            barrier, inc=1, device_id={"head": peer(slot)}, device_id_type=pl.DeviceIdType.MESH
+        )
+    loads = [
+        pltpu.make_async_copy(a, b, load_sem.at[k])
+        for k, (a, b) in enumerate(((out_weight_ref, out_weight), (up_ref, up), (down_ref, down)))
+    ]
+    for load in loads:
+        load.start()
+    pl.semaphore_wait(barrier, heads - 1)
+
+    def to_head(slot):
+        return pltpu.make_async_remote_copy(
+            src_ref=attended_ref.at[peer(slot)], dst_ref=received.at[me],
+            send_sem=send.at[slot], recv_sem=recv.at[slot],
+            device_id={"head": peer(slot)}, device_id_type=pl.DeviceIdType.MESH,
+        )
+
+    for slot in range(1, heads):
+        to_head(slot).start()
+    received[me] = attended_ref[me]
+    for slot in range(1, heads):
+        to_head(slot).wait_recv()
+    for g in range(heads // 2):
+        a, b = received[2 * g], received[2 * g + 1]
+        columns = pl.ds(g * 2 * HD, 2 * HD)
+        gathered[:half, columns] = jnp.concatenate([a[:, :HD], b[:, :HD]], axis=1)
+        gathered[half:, columns] = jnp.concatenate([a[:, HD:], b[:, HD:]], axis=1)
+    loads[0].wait()
+
+    @pl.loop(0, D // FF_BLOCK)
+    def _(j):
+        at = pl.ds(pl.multiple_of(j * FF_BLOCK, FF_BLOCK), FF_BLOCK)
+        residual[:, at] = features_ref[:, at].astype(jnp.float32) + jnp.dot(
+            gathered[...], out_weight[:, at], preferred_element_type=jnp.float32
+        )
+
+    @pl.loop(0, 2 * half // 32)
+    def _(i):
+        at = pl.ds(pl.multiple_of(i * 32, 32), 32)
+        normed[at, :] = layer_norm(residual[at, :], gain_ref[...]).astype(jnp.bfloat16)
+
+    loads[1].wait()
+    loads[2].wait()
+
+    @pl.loop(0, up.shape[1] // FF_BLOCK)
+    def _(j):
+        at = pl.ds(pl.multiple_of(j * FF_BLOCK, FF_BLOCK), FF_BLOCK)
+        hidden = jax.nn.gelu(
+            jnp.dot(normed[...], up[:, at], preferred_element_type=jnp.float32)
+        ).astype(jnp.bfloat16)
+        residual[...] += jnp.dot(hidden, down[at, :], preferred_element_type=jnp.float32)
+
+    updated_ref[...] = residual[...].astype(jnp.bfloat16)
+    for slot in range(1, heads):
+        to_head(slot).wait_send()
+
+
+def finish(attended, features, gain, out_weight, up, down):
+    heads = attended.shape[0]
+    rows = features.shape[0]
+    vmem = pl.BlockSpec(memory_space=pltpu.VMEM)
+    hbm = pl.BlockSpec(memory_space=pl.ANY)
+    dma = pltpu.SemaphoreType.DMA
+    return pl.pallas_call(
+        finish_kernel,
+        out_shape=jax.ShapeDtypeStruct((rows, D), jnp.bfloat16),
+        in_specs=[vmem, vmem, vmem, hbm, hbm, hbm],
+        out_specs=vmem,
+        scratch_shapes=[
+            pltpu.VMEM(out_weight.shape, jnp.bfloat16),
+            pltpu.VMEM(up.shape, jnp.bfloat16),
+            pltpu.VMEM(down.shape, jnp.bfloat16),
+            pltpu.VMEM(attended.shape, jnp.bfloat16),
+            pltpu.VMEM((rows, D), jnp.bfloat16),
+            pltpu.VMEM((rows, D), jnp.float32),
+            pltpu.VMEM((rows, D), jnp.bfloat16),
+            dma((3,)),
+            dma((heads,)),
+            dma((heads,)),
+        ],
+        compiler_params=pltpu.CompilerParams(
+            collective_id=2, has_side_effects=True, vmem_limit_bytes=67043328
+        ),
+        name="finish",
+    )(attended, features, gain.reshape(1, D), out_weight, up, down)
 
 
 def shards(
@@ -425,30 +549,18 @@
     tile_pattern,
     node_order,
 ):
-    own_rows = features.shape[0]
     partitions = lax.axis_size("node")
-    rows_part = own_rows * lax.axis_size("head")
-    query_tiles = rows_part // TILE
-    weight = qkv_weight[:, 0].T
-    weight = jnp.concatenate([weight[HD:], weight[:HD]], 0).reshape(2, HALF, D)
+    heads = lax.axis_size("head")
+    query_tiles = features.shape[0] * heads // TILE
+    weight = qkv_weight[:, 0].T.reshape(2, HALF, D)
     order = node_order[0]
     window, query = exchange(order, project(features, attn_gain, weight))
     partition = lax.axis_index("node")
     position = (
         tile_pattern // query_tiles - partition + REACH + partitions
     ) % partitions * query_tiles + tile_pattern % query_tiles
-    restored = attention(position, order, query, window)
-    gathered_heads = lax.all_to_all(restored, "head", split_axis=0, concat_axis=1, tiled=True)
-    residual = features.astype(jnp.float32) + jnp.dot(
-        gathered_heads, out_weight, preferred_element_type=jnp.float32
-    )
-    mlp_input = layer_norm(residual, feedforward_norm_gain).astype(jnp.bfloat16)
-    hidden = jax.nn.gelu(jnp.dot(mlp_input, up_weight, preferred_element_type=jnp.float32)).astype(
-        jnp.bfloat16
-    )
-    return (residual + jnp.dot(hidden, down_weight, preferred_element_type=jnp.float32)).astype(
-        jnp.bfloat16
-    )
+    attended = attention(position, order, query, window, heads)
+    return finish(attended, features, feedforward_norm_gain, out_weight, up_weight, down_weight)
 
 
 def solution(mesh):

time: 137 us -> 126 us (0.920)
  Pallas kernels: 103 us -> 122 us
  blocking collectives: 17.9 us -> 0 us
  matrix products: 8.82 us -> 0 us
  local copies, waits for them, and re-layouts: 5.68 us -> 2.63 us
    all_to_all x1 -> x0, blocking collectives: 17.9 us -> none  [shards(): lax.all_to_all(restored, 'head', split_axis=0, concat_axis=1, tiled=True)]
    pallas_call x1 -> x2, Pallas kernels: 22.7 us -> 36.2 us  [the longest x1 22 us: finish(): pl.pallas_call(finish_kernel, out_shape=jax.ShapeDtypeStruct((rows, D), j...]
    dot_general x2 -> x0, matrix products: 8.82 us -> none  [the longest x1 6.94 us: shards(): jnp.dot(hidden, down_weight, preferred_element_type=jnp.float32)]
    pallas_call x1, Pallas kernels: 30.6 us -> 33.9 us  [exchange(): pl.pallas_call(exchange_kernel, out_shape=[jax.ShapeDtypeStruct((WINDOW,...]
    pallas_call x1, Pallas kernels: 49.5 us -> 51.9 us  [project(): pl.pallas_call(project_kernel, out_shape=jax.ShapeDtypeStruct((heads, row...]
    slice x2 -> x0, local copies, waits for them, and re-layouts: 2.05 us -> none  [shards(): weight = jnp.concatenate([weight[HD:], weight[:HD]], 0).reshape(2, HALF, D)]
where the time goes in v3:
time: 126 us; the launch traced here: 125 us
  Pallas kernels  122 us (97%)
  local copies, waits for them, and re-layouts  2.63 us (2%)
    pallas_call x1, Pallas kernels, project(): pl.pallas_call(project_kernel, out_shape=jax.ShapeDtypeStruct((heads, row...  51.9 us
    pallas_call x1, Pallas kernels, exchange(): pl.pallas_call(exchange_kernel, out_shape=[jax.ShapeDtypeStruct((WINDOW,...  33.9 us
    pallas_call x1, Pallas kernels, finish(): pl.pallas_call(finish_kernel, out_shape=jax.ShapeDtypeStruct((rows, D), j...  22 us
    pallas_call x1, Pallas kernels, attention(): pl.pallas_call(attention_kernel, out_shape=jax.ShapeDtypeStruct((heads, n...  14.2 us
    unnamed x2, local copies, waits for them, and re-layouts  2.63 us

profile of v3, /device:TPU:96, one launch (start us, length us, event | category | flops | bytes accessed | tf_op | source)
XLA Modules:
  0.0 125.2 jit_solution(4315490237746233980)
XLA Ops:
  0.0 51.9 %project.1.rows_ref = bf16[16,384,128]{2,1,0:T(8,128)(2,1)} custom-call(bf16[256,1024]{1,0:T(8,128)(2,1)} %features_ref.3, f32[1,1024]{1,0:T(1,128)} %bitcast.13, bf16[2,96,1024]{2,1,0:T(8,128)(2,1)} %bitcast.10), custom_call_target="tpu_custom_call" | custom-call | tf_op jit(solution)/shard_map/project/pallas_call | solution.py:222
  51.9 33.9 %exchange.1 = (bf16[5,32,128,128]{3,2,1,0:T(8,128)(2,1)}, bf16[4096,128]{1,0:T(8,128)(2,1)}) custom-call(s32[4096]{0:T(1024)} %bitcast.11, bf16[16,384,128]{2,1,0:T(8,128)(2,1)} %project.1.rows_ref), custom_call_target="tpu_custom_call" | custom-call | tf_op jit(solution)/shard_map/exchange/pallas_call | solution.py:350
  85.7 0.8 copy.10
  86.5 0.6 fusion.4.position_ref
  87.1 14.2 %attention.1.attended_ref = bf16[16,128,128]{2,1,0:T(8,128)(2,1)} custom-call(s32[32,8]{1,0:T(8,128)} %fusion.4.position_ref, s32[4096]{0:T(1024)} %bitcast.12, bf16[4096,128]{1,0:T(8,128)(2,1)} %get-tuple-element.7.query_ref, bf16[160,128,128]{2,1,0:T(8,128)(2,1)} %bitcast.9), custom_call_target="tpu_custom_call" | custom-call | tf_op jit(solution)/shard_map/attention/pallas_call | solution.py:423
  101.3 22.0 %finish.1 = bf16[256,1024]{1,0:T(8,128)(2,1)} custom-call(bf16[16,128,128]{2,1,0:T(8,128)(2,1)} %attention.1.attended_ref, bf16[256,1024]{1,0:T(8,128)(2,1)} %features_ref.3, f32[1,1024]{1,0:T(1,128)} %bitcast.14, bf16[1024,1024]{1,0:T(8,128)(2,1)} %out_weight_ref.1, bf16[1024,2048]{1,0:T(8,128)(2,1)} %up_ref.1, bf16[2048,1024]{1,0:T(8,128)(2,1)} %down_ref.1), custom_call_target="tpu_custom_call" | custom-call | tf_op jit(solution)/shard_map/finish/pallas_call | solution.py:517
  123.3 1.9 %copy.15 = bf16[256,1024]{1,0:T(8,128)(2,1)} copy(bf16[256,1024]{1,0:T(8,128)(2,1)} %finish.1) | data formatting | bytes 1048576
